TPU v7x, 256 devices: a whole 4x4x8 slice. The times are simulated.
256 devices in a mesh: src: 16 (over x_lo, y, core), rcv: 16 (over z, x_hi).
Axes of the slice: x: 4 (x_hi: 2, x_lo: 2; x = x_hi * 2 + x_lo), y: 4, z: 8, core: 2. Of those that a mesh axis runs over, the one named last changes fastest.
Arguments:
- recorded: bfloat16 [2, 16384, 16384], P(None, 'src', 'rcv'), may hold values from -6 to 6
- obliquity: float32 [16, 1024], replicated, may hold values from 0.01 to 0.25
- clip_level: float32 [16384], P('src'), may hold values from 0.3 to 3
Outputs:
- first_pass: bfloat16 [2, 16384, 16384], P(None, 'src', 'rcv')
- primaries: bfloat16 [2, 16384, 16384], P(None, 'src', 'rcv')
All inputs are finite; a program needn't handle non-finite values.
Results may differ from a plain program's by a relative error of at most 0.0025.
Values may be sent and summed in bfloat16 or wider, within the bound.
A program may use at most 128 MiB of HBM per device.

v0:
```python
import math
import jax
import jax.numpy as jnp
from jax import lax
from jax.sharding import PartitionSpec as P

N = 16384
K = 256
TWO_PI = 2.0 * math.pi


def rotate(real_part, imag_part, cosine, sine_part):
    return (real_part * cosine - imag_part * sine_part, real_part * sine_part + imag_part * cosine)


def twiddle(real_part, imag_part, column_index, group_index, orient, total_length):
    angles = (column_index * group_index % total_length).astype(jnp.float32) * (
        TWO_PI / total_length
    )
    return rotate(real_part, imag_part, jnp.cos(angles), orient * jnp.sin(angles))


def long_table(length, orient):
    index_left = lax.broadcasted_iota(jnp.int32, (length, length), 0)
    index_right = lax.broadcasted_iota(jnp.int32, (length, length), 1)
    angles = (index_left * index_right % length).astype(jnp.float32) * (TWO_PI / length)
    cosine = jnp.cos(angles)
    sine_part = orient * jnp.sin(angles)
    upper = jnp.concatenate([cosine, sine_part], axis=1)
    lower = jnp.concatenate([-sine_part, cosine], axis=1)
    return jnp.concatenate([upper, lower], axis=0)


def long_transform(real_part, imag_part, orient):
    length = real_part.shape[-1]
    joined = jnp.concatenate([real_part, imag_part], axis=-1)
    result = jnp.dot(
        joined.reshape(-1, 2 * length),
        long_table(length, orient),
        precision=lax.Precision.HIGHEST,
        preferred_element_type=jnp.float32,
    )
    result = result.reshape(joined.shape)
    return (result[..., :length], result[..., length:])


def across_groups(real_part, imag_part, groups, orient):
    index_left = lax.broadcasted_iota(jnp.int32, (groups, groups), 0)
    index_right = lax.broadcasted_iota(jnp.int32, (groups, groups), 1)
    angles = (index_left * index_right % groups).astype(jnp.float32) * (TWO_PI / groups)
    cosine = jnp.cos(angles)
    sine_part = orient * jnp.sin(angles)
    highest = lax.Precision.HIGHEST
    new_real = jnp.einsum("mgc,gk->mkc", real_part, cosine, precision=highest) - jnp.einsum(
        "mgc,gk->mkc", imag_part, sine_part, precision=highest
    )
    new_imag = jnp.einsum("mgc,gk->mkc", real_part, sine_part, precision=highest) + jnp.einsum(
        "mgc,gk->mkc", imag_part, cosine, precision=highest
    )
    return (new_real, new_imag)


def filter_rows(whole_rows, obliquity, groups):
    row_total = whole_rows.shape[1]
    group_cols = whole_rows.shape[2] // groups
    total_length = groups * group_cols
    values = whole_rows.astype(jnp.float32).reshape(2, row_total, groups, group_cols)
    real_part, imag_part = across_groups(values[0], values[1], groups, -1.0)
    column_index = lax.broadcasted_iota(jnp.int32, (1, 1, group_cols), 2)
    group_index = lax.broadcasted_iota(jnp.int32, (1, groups, 1), 1)
    real_part, imag_part = twiddle(
        real_part, imag_part, column_index, group_index, -1.0, total_length
    )
    real_part, imag_part = long_transform(real_part, imag_part, -1.0)
    real_part = real_part * obliquity[None]
    imag_part = imag_part * obliquity[None]
    real_part, imag_part = long_transform(real_part, imag_part, 1.0)
    real_part, imag_part = twiddle(
        real_part, imag_part, column_index, group_index, 1.0, total_length
    )
    real_part, imag_part = across_groups(real_part, imag_part, groups, 1.0)
    inverse_scale = 1.0 / total_length
    returned = jnp.stack([real_part * inverse_scale, imag_part * inverse_scale])
    return returned.reshape(2, row_total, total_length).astype(jnp.bfloat16)


def through_rows(panel_rows, obliquity):
    moved_rows = lax.all_to_all(panel_rows, "rcv", split_axis=1, concat_axis=2, tiled=True)
    returned = filter_rows(moved_rows, obliquity, lax.axis_size("rcv"))
    return lax.all_to_all(returned, "rcv", split_axis=2, concat_axis=1, tiled=True)


def complex_product(left_rows, right_rows):
    left_joined = jnp.concatenate([left_rows[0], left_rows[1]], axis=0)
    upper = jnp.concatenate([right_rows[0], right_rows[1]], axis=1)
    lower = jnp.concatenate([-right_rows[1], right_rows[0]], axis=1)
    right_joined = jnp.concatenate([upper, lower], axis=0)
    return lax.dot_general(
        left_joined, right_joined, (((0,), (0,)), ((), ())), preferred_element_type=jnp.float32
    )


def per_device(recorded, obliquity, clip_level):
    spacing = N // K
    row_total = recorded.shape[1]
    col_total = recorded.shape[2]
    panel_rows = recorded.reshape(2, row_total // spacing, spacing, col_total)[:, :, 0, :]
    filtered = through_rows(panel_rows, obliquity)
    clip_rows = clip_level[:, None]
    estimate = recorded
    passes = []
    for update_index in range(2):
        columns = estimate.reshape(2, row_total, col_total // spacing, spacing)[:, :, :, 0]
        left_local = jnp.swapaxes(columns, 1, 2)
        left_panel = lax.all_gather(left_local, "rcv", axis=1, tiled=True)

        def accumulate(running, panel_piece, first_row, left_all=left_panel):
            return complex_product(left_all, panel_piece)

        zeros_init = jnp.zeros((row_total, 2 * col_total), jnp.float32)
        product_sum = accumulate(
            zeros_init, lax.all_gather(filtered, "src", axis=1, tiled=True), jnp.int32(0)
        )
        pred_real = product_sum[:, :col_total]
        pred_imag = product_sum[:, col_total:]
        limiter = lax.rsqrt(
            1.0 + (pred_real * pred_real + pred_imag * pred_imag) / (clip_rows * clip_rows)
        )
        estimate = (
            recorded.astype(jnp.float32) - jnp.stack([pred_real * limiter, pred_imag * limiter])
        ).astype(jnp.bfloat16)
        passes.append(estimate)
    return (passes[0], passes[1])


def solution(mesh):
    return jax.shard_map(
        per_device,
        mesh=mesh,
        in_specs=(P(None, "src", "rcv"), P(), P("src")),
        out_specs=(P(None, "src", "rcv"), P(None, "src", "rcv")),
        check_vma=False,
    )
```

profile of v0, /device:TPU:8, one launch (start us, length us, event | category | flops | bytes accessed | tf_op | source)
XLA Modules:
  0.0 447.1 jit_solution(7777668069207956827)
XLA Ops:
  7.2 1.1 slice.88
  8.3 0.7 copy.65
  9.0 11.0 %all-to-all-start = ((bf16[2,16,1024]{2,0,1:T(2,128)(2,1)}), bf16[2,16,1024]{2,0,1:T(2,128)(2,1)S(1)}, u32[]{:S(2)}, u32[]{:S(2)}) async-start(bf16[2,16,1024]{2,0,1:T(2,128)(2,1)} %bitcast.83), calls=%async_computation | async-start | bytes 131072 | tf_op jit(solution)/shard_map/all_to_all | solution.py:88
  20.1 0.0 all-gather.4.cloned.1.call-start
  20.1 6.2 %copy.36 = bf16[2,1024,1024]{1,2,0:T(8,128)(2,1)} copy(bf16[2,1024,1024]{2,1,0:T(8,128)(2,1)} %param.3) | data formatting | bytes 8388608 | tf_op args[0]
  26.3 1.1 slice.85
  27.4 0.7 copy.64
  28.1 0.0 all-gather.4.cloned.1.call-update
  28.1 0.0 all-gather.6.cloned.1.call-start
  28.2 17.6 %broadcast_multiply_fusion = (f32[1024,1024]{1,0:T(8,128)}, f32[1024,1024]{1,0:T(8,128)}) fusion(), kind=kLoop, calls=%fused_computation.35 | loop fusion | flops 15728640 | bytes 8388608 | tf_op jit(solution)/shard_map/mul | solution.py:28
  45.8 16.3 %fusion.27 = f32[1024,1024]{1,0:T(8,128)} fusion(), kind=kLoop, calls=%fused_computation.39 | loop fusion | flops 16777216 | bytes 4194304 | tf_op jit(solution)/shard_map/neg | solution.py:30
  62.1 16.7 %fusion.24 = (f32[1024,1024]{1,0:T(8,128)}, f32[1024,1024]{1,0:T(8,128)}) fusion(), kind=kLoop, calls=%fused_computation.36 | loop fusion | flops 15728640 | bytes 8388608 | tf_op jit(solution)/shard_map/sin | solution.py:28
  78.8 0.0 all-to-all-done
  78.9 0.1 fusion.138
  79.0 0.3 fusion.65
  79.2 0.3 fusion.66
  79.5 0.3 convolution_add_fusion.1
  79.8 0.5 subtract_bitcast_fusion
  80.3 0.0 copy-start.2
  80.3 13.8 %fusion.21 = f32[1,16,2048]{2,1,0:T(8,128)S(1)} fusion(f32[1024,1024]{1,0:T(8,128)} %get-tuple-element.19, f32[1024,1024]{1,0:T(8,128)} %fusion.27, f32[1024,1024]{1,0:T(8,128)} %get-tuple-element.18, f32[1,16,1024]{2,1,0:T(8,128)S(1)} %get-tuple-element.15, f32[1,16,1024]{2,1,0:T(8,128)S(1)} %get-tuple-element.14), kind=kOutput, calls=%fused_computation.33 | convolution fusion | flops 817922048 | bytes 12845056 | tf_op jit(solution)/shard_map/dot_general | solution.py:37
  94.1 0.0 copy-done.2
  94.2 14.0 %fusion.18 = f32[1,16,2048]{2,1,0:T(8,128)S(1)} fusion(f32[1024,1024]{1,0:T(8,128)} %get-tuple-element.19, f32[1024,1024]{1,0:T(8,128)} %get-tuple-element.21, f32[1024,1024]{1,0:T(8,128)} %get-tuple-element.20, f32[1,16,1024]{2,1,0:T(8,128)S(1)} %get-tuple-element.13, f32[1,16,1024]{2,1,0:T(8,128)S(1)} %get-tuple-element.12), kind=kOutput, calls=%fused_computation.32 | convolution fusion | flops 817922048 | bytes 12845056 | tf_op jit(solution)/shard_map/dot_general | solution.py:37
  108.2 0.5 fusion.54
  108.7 0.5 fusion.30
  109.2 0.5 fusion.52
  109.7 11.5 %stack.36 = bf16[1,1,16384]{0,1,2:T(2,128)(2,1)} reshape(bf16[16,1024]{1,0:T(8,128)(2,1)S(1)} %fusion.30) | data formatting | bytes 65536 | tf_op jit(solution)/shard_map/stack | solution.py:83
  121.2 0.5 fusion.31
  121.7 12.0 %stack.37 = bf16[1,1,16384]{0,1,2:T(2,128)(2,1)} reshape(bf16[16,1024]{1,0:T(8,128)(2,1)S(1)} %fusion.31) | data formatting | bytes 65536 | tf_op jit(solution)/shard_map/stack | solution.py:83
  133.6 25.2 %fusion.139 = bf16[16384,1,2]{2,1,0:T(2,128)(2,1)} fusion(bf16[1,1,16384]{0,1,2:T(2,128)(2,1)} %stack.37, bf16[1,1,16384]{0,1,2:T(2,128)(2,1)} %stack.36), kind=kLoop, calls=%fused_computation.177 | loop fusion | flops 131072 | bytes 131072
  158.8 0.5 broadcast.277
  159.4 90.8 %reduce = bf16[16384,2]{1,0:T(8,128)(2,1)} reduce(bf16[16384,1,2]{2,1,0:T(2,128)(2,1)} %fusion.139, bf16[]{:T(256)} %broadcast.277), dimensions={1}, to_apply=%fusion.139.reduce_sub_computation | reduce | bytes 131074
  250.2 7.2 %reshape.220 = bf16[16,2,1024]{2,1,0:T(2,128)(2,1)S(1)} reshape(bf16[16384,2]{1,0:T(8,128)(2,1)} %reduce) | data formatting | bytes 131072
  257.3 20.0 %all_to_all.21 = bf16[16,2,1024]{2,1,0:T(2,128)(2,1)S(1)} all-to-all(bf16[16,2,1024]{2,1,0:T(2,128)(2,1)S(1)} %reshape.220), channel_id=1, replica_groups=mesh['src'=16,'rcv'=16] {'rcv'}, dimensions={0} | all-to-all | bytes 131072 | tf_op jit(solution)/shard_map/all_to_all | solution.py:90
  277.3 11.9 %reshape.221 = bf16[16384,1,2]{2,1,0:T(2,128)(2,1)} reshape(bf16[16,2,1024]{2,1,0:T(2,128)(2,1)S(1)} %all_to_all.21) | data formatting | bytes 131072
  289.2 0.0 copy-start.3
  289.2 15.4 %copy.42 = bf16[2,1,16384]{2,0,1:T(2,128)(2,1)S(1)} copy(bf16[2,1,16384]{0,1,2:T(2,128)(2,1)} %bitcast.85) | data formatting | bytes 131072 | tf_op jit(solution)/shard_map/all_to_all | solution.py:90
  304.6 0.7 copy.62
  305.2 0.0 all-gather.6.cloned.1.call-update
  305.3 0.2 all-gather.8.cloned.1.call-start
  305.5 0.0 copy-done.3
  305.5 0.0 all-gather.4.cloned.1.call-done
  305.5 1.3 slice_bitcast_fusion.5
  306.8 26.9 %all-gather.6.cloned.1.call-done = bf16[2,256,1024]{2,1,0:T(8,128)(2,1)} async-done(((bf16[2,16,1024]{2,1,0:T(8,128)(2,1)}), bf16[2,256,1024]{2,1,0:T(8,128)(2,1)}) %all-gather.6.cloned.1.call-update) | async-done | bytes 1048592 | tf_op jit(solution)/shard_map/all_gather | solution.py:122
  333.7 1.3 slice_bitcast_fusion.2
  335.0 1.1 fusion.137
  336.1 2.4 fusion.32
  338.5 0.0 copy-start
  338.5 2.4 multiply_bitcast_fusion.3
  340.9 0.0 copy-done
  340.9 3.0 fusion.10
  343.9 6.2 %copy.43 = bf16[2,1024,1024]{1,2,0:T(8,128)(2,1)} copy(bf16[2,1024,1024]{2,1,0:T(8,128)(2,1)} %fusion.10) | data formatting | bytes 8388608 | tf_op jit(solution)/shard_map/convert_element_type | solution.py:131
  350.1 1.1 slice.99
  351.2 0.7 copy.63
  351.9 0.0 all-gather.8.cloned.1.call-update
  351.9 79.3 %all-gather.8.cloned.1.call-done = bf16[2,256,1024]{2,1,0:T(8,128)(2,1)} async-done(((bf16[2,16,1024]{2,1,0:T(8,128)(2,1)}), bf16[2,256,1024]{2,1,0:T(8,128)(2,1)}) %all-gather.8.cloned.1.call-update) | async-done | bytes 1048592 | tf_op jit(solution)/shard_map/all_gather | solution.py:115
  431.3 1.3 slice_bitcast_fusion.1
  432.5 2.4 fusion.36
  434.9 0.0 copy-start.1
  435.0 2.4 multiply_bitcast_fusion.1
  437.4 0.0 copy-done.1
  437.4 3.0 fusion.11
  (2 shorter events, 0.0 us)
Async XLA Ops:
  9.0 69.8 %all-to-all-start = ((bf16[2,16,1024]{2,0,1:T(2,128)(2,1)}), bf16[2,16,1024]{2,0,1:T(2,128)(2,1)S(1)}, u32[]{:S(2)}, u32[]{:S(2)}) async-start(bf16[2,16,1024]{2,0,1:T(2,128)(2,1)} %bitcast.83), calls=%async_computation | async-start | bytes 131072 | tf_op jit(solution)/shard_map/all_to_all | solution.py:88
  20.1 285.5 %all-gather.4.cloned.1.call-start = ((), (), s32[]{:S(2)}) async-start(), calls=%async_computation.2 | async-start | bytes 1114112 | tf_op jit(solution)/shard_map/all_gather | solution.py:115
  28.1 305.6 %all-gather.6.cloned.1.call-start = ((), (), s32[]{:S(2)}) async-start(), calls=%async_computation.3 | async-start | bytes 1114112 | tf_op jit(solution)/shard_map/all_gather | solution.py:122
  80.3 13.9 %copy-start.2 = (f32[16,1024]{1,0:T(8,128)S(1)}, f32[16,1024]{1,0:T(8,128)}, u32[]{:S(2)}) copy-start(f32[16,1024]{1,0:T(8,128)} %param.4) | copy-start | bytes 196612
  289.2 16.3 %copy-start.3 = (f32[1024]{0:T(1024)S(1)}, f32[1024]{0:T(1024)}, u32[]{:S(2)}) copy-start(f32[1024]{0:T(1024)} %param.5) | copy-start | bytes 12292
  305.3 126.0 %all-gather.8.cloned.1.call-start = ((), (), s32[]{:S(2)}) async-start(), calls=%async_computation.4 | async-start | bytes 1114112 | tf_op jit(solution)/shard_map/all_gather | solution.py:115
  338.5 2.5 copy-start
  434.9 2.5 copy-start.1
Sparse Core Ops, SparseCore 0:
  28.2 80.2 all-gather.3
  305.4 28.2 all-gather.5
  352.0 79.1 all-gather.7
where the time goes:
time: 452 us; the launch traced here: 447 us
  other arithmetic  179 us (40%)
  waiting for transfers between devices  106 us (23%)
  local copies, waits for them, and re-layouts  80.7 us (18%)
  matrix products  35.9 us (8%)
  blocking collectives  20 us (4%)
  between operations  14.2 us (3%)
  starting transfers between devices  11.3 us (2%)
    unnamed x2, other arithmetic  116 us
    all_gather x2, waiting for transfers between devices, per_device(): left_panel = lax.all_gather(left_local, 'rcv', axis=1, tiled=True)  79.4 us
    dot_general x2, matrix products, long_transform(): jnp.dot(joined.reshape(-1, 2 * length), long_table(length, orient), preci...  27.9 us
    unnamed x15, local copies, waits for them, and re-layouts  27.8 us
    all_gather x1, waiting for transfers between devices, per_device(): lax.all_gather(filtered, 'src', axis=1, tiled=True)  26.9 us
    another operation x2, local copies, waits for them, and re-layouts, filter_rows(): returned = jnp.stack([real_part * inverse_scale, imag_part * inverse_scale])  23.4 us
    all_to_all x1, blocking collectives, through_rows(): lax.all_to_all(returned, 'rcv', split_axis=2, concat_axis=1, tiled=True)  20 us
    mul x1, other arithmetic, long_table(): sine_part = orient * jnp.sin(angles)  17.6 us
  transfers between devices with their start and end apart: 4, of which 2 were waited for; matrix products, arithmetic and copies ran while one was open for 60% of the time, Pallas kernels for 0%

commit v1 on v0

--- a/solution.py
+++ b/solution.py
@@ -87,7 +87,10 @@
 def through_rows(panel_rows, obliquity):
     moved_rows = lax.all_to_all(panel_rows, "rcv", split_axis=1, concat_axis=2, tiled=True)
     returned = filter_rows(moved_rows, obliquity, lax.axis_size("rcv"))
-    return lax.all_to_all(returned, "rcv", split_axis=2, concat_axis=1, tiled=True)
+    return jnp.concatenate(
+        lax.all_to_all(jnp.stack(jnp.split(returned, lax.axis_size("rcv"), axis=2)), "rcv", 0, 0),
+        axis=1,
+    )
 
 
 def complex_product(left_rows, right_rows):

time: 452 us -> 274 us (0.61); the launches traced: 447 us -> 274 us
  other arithmetic: 179 us -> 62 us
  local copies, waits for them, and re-layouts: 80.7 us -> 24 us
    unnamed x2 -> x15, other arithmetic: 116 us -> 0.33 us
    another operation x2, local copies, waits for them, and re-layouts: 23.4 us -> 0.06 us  [filter_rows(): returned = jnp.stack([real_part * inverse_scale, imag_part * inverse_scale])]
    unnamed x15 -> x12, local copies, waits for them, and re-layouts: 27.8 us -> 7.69 us
    all_to_all x1 -> x0, local copies, waits for them, and re-layouts: 15.4 us -> none  [through_rows(): lax.all_to_all(returned, 'rcv', split_axis=2, concat_axis=1, tiled=True)]
  transfers between devices with their start and end apart: 4 -> 4, of which waited for: 2 -> 2; matrix products, arithmetic and copies ran while one was open for 60% -> 33% of each run, Pallas kernels for 0% -> 0%
where the time goes in v1:
time: 274 us
  waiting for transfers between devices  106 us (39%)
  other arithmetic  62 us (23%)
  matrix products  36 us (13%)
  local copies, waits for them, and re-layouts  24 us (9%)
  blocking collectives  20.1 us (7%)
  between operations  14 us (5%)
  starting transfers between devices  11.2 us (4%)
    all_gather x2, waiting for transfers between devices, per_device(): left_panel = lax.all_gather(left_local, 'rcv', axis=1, tiled=True)  79.3 us
    dot_general x2, matrix products, long_transform(): jnp.dot(joined.reshape(-1, 2 * length), long_table(length, orient), preci...  27.9 us
    all_gather x1, waiting for transfers between devices, per_device(): lax.all_gather(filtered, 'src', axis=1, tiled=True)  27.1 us
    all_to_all x1, blocking collectives, through_rows(): lax.all_to_all(jnp.stack(jnp.split(returned, lax.axis_size('rcv'), axis=2...  20.1 us
    mul x1, other arithmetic, long_table(): sine_part = orient * jnp.sin(angles)  17.6 us
    sin x1, other arithmetic, long_table(): sine_part = orient * jnp.sin(angles)  16.6 us
    neg x1, other arithmetic, long_table(): lower = jnp.concatenate([-sine_part, cosine], axis=1)  16.3 us
    all_to_all x1, starting transfers between devices, through_rows(): lax.all_to_all(panel_rows, 'rcv', split_axis=1, concat_axis=2, tiled=True)  11 us
  transfers between devices with their start and end apart: 4, of which 2 were waited for; matrix products, arithmetic and copies ran while one was open for 33% of the time, Pallas kernels for 0%

profile of v1, /device:TPU:8, one launch (start us, length us, event | category | flops | bytes accessed | tf_op | source)
XLA Modules:
  0.0 273.7 jit_solution(16101101903672011770)
XLA Ops:
  7.2 1.1 slice.90
  8.3 0.7 copy.69
  9.0 11.0 %all-to-all-start = ((bf16[2,16,1024]{2,0,1:T(2,128)(2,1)}), bf16[2,16,1024]{2,0,1:T(2,128)(2,1)S(1)}, u32[]{:S(2)}, u32[]{:S(2)}) async-start(bf16[2,16,1024]{2,0,1:T(2,128)(2,1)} %bitcast.141), calls=%async_computation | async-start | bytes 131072 | tf_op jit(solution)/shard_map/all_to_all | solution.py:88
  20.0 0.0 all-gather.5.cloned.1.call-start
  20.1 6.2 %copy.36 = bf16[2,1024,1024]{1,2,0:T(8,128)(2,1)} copy(bf16[2,1024,1024]{2,1,0:T(8,128)(2,1)} %param.3) | data formatting | bytes 8388608 | tf_op args[0]
  26.3 1.1 slice.87
  27.4 0.6 copy.68
  28.1 0.0 all-gather.5.cloned.1.call-update
  28.1 0.0 all-gather.9.cloned.1.call-start
  28.1 17.6 %broadcast_multiply_fusion = (f32[1024,1024]{1,0:T(8,128)}, f32[1024,1024]{1,0:T(8,128)}) fusion(), kind=kLoop, calls=%fused_computation.34 | loop fusion | flops 15728640 | bytes 8388608 | tf_op jit(solution)/shard_map/mul | solution.py:28
  45.8 16.3 %fusion.27 = f32[1024,1024]{1,0:T(8,128)} fusion(), kind=kLoop, calls=%fused_computation.38 | loop fusion | flops 16777216 | bytes 4194304 | tf_op jit(solution)/shard_map/neg | solution.py:30
  62.1 16.6 %fusion.24 = (f32[1024,1024]{1,0:T(8,128)}, f32[1024,1024]{1,0:T(8,128)}) fusion(), kind=kLoop, calls=%fused_computation.35 | loop fusion | flops 15728640 | bytes 8388608 | tf_op jit(solution)/shard_map/sin | solution.py:28
  78.7 0.0 all-to-all-done
  78.7 0.1 fusion.140
  78.8 0.3 fusion.65
  79.0 0.3 fusion.66
  79.3 0.3 convolution_add_fusion.1
  79.6 0.5 subtract_bitcast_fusion
  80.1 0.0 copy-start.2
  80.1 13.8 %fusion.21 = f32[1,16,2048]{2,1,0:T(8,128)S(1)} fusion(f32[1024,1024]{1,0:T(8,128)} %get-tuple-element.21, f32[1024,1024]{1,0:T(8,128)} %fusion.27, f32[1024,1024]{1,0:T(8,128)} %get-tuple-element.20, f32[1,16,1024]{2,1,0:T(8,128)S(1)} %get-tuple-element.17, f32[1,16,1024]{2,1,0:T(8,128)S(1)} %get-tuple-element.16), kind=kOutput, calls=%fused_computation.32 | convolution fusion | flops 817922048 | bytes 12845056 | tf_op jit(solution)/shard_map/dot_general | solution.py:37
  93.9 0.0 copy-done.2
  94.0 0.0 copy-start.3
  94.0 14.1 %fusion.18 = f32[1,16,2048]{2,1,0:T(8,128)S(1)} fusion(f32[1024,1024]{1,0:T(8,128)} %get-tuple-element.21, f32[1024,1024]{1,0:T(8,128)} %get-tuple-element.23, f32[1024,1024]{1,0:T(8,128)} %get-tuple-element.22, f32[1,16,1024]{2,1,0:T(8,128)S(1)} %get-tuple-element.15, f32[1,16,1024]{2,1,0:T(8,128)S(1)} %get-tuple-element.14), kind=kOutput, calls=%fused_computation.31 | convolution fusion | flops 817922048 | bytes 12845056 | tf_op jit(solution)/shard_map/dot_general | solution.py:37
  108.0 0.5 fusion.54
  108.5 0.5 fusion.52
  109.0 0.5 fusion.30
  109.5 0.5 fusion.31
  110.5 20.1 %all_to_all.14 = bf16[16,2,1,1024]{3,1,2,0:T(2,128)(2,1)} all-to-all(bf16[16,2,1,1024]{3,1,2,0:T(2,128)(2,1)S(1)} %constant_dynamic-update-slice_fusion), channel_id=1, replica_groups=mesh['src'=16,'rcv'=16] {'rcv'}, dimensions={0} | all-to-all | bytes 131072 | tf_op jit(solution)/shard_map/all_to_all | solution.py:91
  130.6 0.0 all-gather.9.cloned.1.call-update
  130.6 0.0 all-gather.7.cloned.1.call-start
  130.6 0.0 copy-done.3
  130.7 0.0 all-gather.5.cloned.1.call-done
  130.7 1.3 slice_bitcast_fusion.3
  132.0 27.1 %all-gather.9.cloned.1.call-done = bf16[2,256,1,1024]{3,0,2,1:T(2,128)(2,1)} async-done(((bf16[2,16,1,1024]{3,0,2,1:T(2,128)(2,1)}), bf16[2,256,1,1024]{3,0,2,1:T(2,128)(2,1)}) %all-gather.9.cloned.1.call-update) | async-done | bytes 1048592 | tf_op jit(solution)/shard_map/all_gather | solution.py:125
  159.1 3.4 %fusion.139 = (bf16[1,256,1,1024]{3,0,2,1:T(2,128)(2,1)S(1)}, bf16[1,256,1,1024]{3,0,2,1:T(2,128)(2,1)S(1)}) fusion(bf16[2,256,1,1024]{3,0,2,1:T(2,128)(2,1)} %all-gather.9.cloned.1.call-done), kind=kLoop, calls=%fused_computation.207 | loop fusion | bytes 2097152 | tf_op jit(solution)/shard_map/slice | solution.py:98
  162.4 0.2 fusion.138
  162.6 0.2 copy.66
  162.8 2.4 fusion.32
  165.2 0.0 copy-start
  165.2 2.4 multiply_bitcast_fusion.3
  167.7 0.0 copy-done
  167.7 3.0 %fusion.10 = bf16[2,1024,1024]{2,1,0:T(8,128)(2,1)} fusion(bf16[2,1024,1024]{2,1,0:T(8,128)(2,1)S(1)} %copy-done, f32[1,1024,1024]{2,1,0:T(8,128)S(1)} %get-tuple-element.7, f32[1,1024,1024]{2,1,0:T(8,128)S(1)} %get-tuple-element.6), kind=kLoop, calls=%fused_computation.14 | loop fusion | flops 8388608 | bytes 16777216 | tf_op jit(solution)/shard_map/convert_element_type | solution.py:134
  170.7 6.2 %copy.44 = bf16[2,1024,1024]{1,2,0:T(8,128)(2,1)} copy(bf16[2,1024,1024]{2,1,0:T(8,128)(2,1)} %fusion.10) | data formatting | bytes 8388608 | tf_op jit(solution)/shard_map/convert_element_type | solution.py:134
  176.9 1.1 slice.101
  178.0 0.7 copy.67
  178.6 0.0 all-gather.7.cloned.1.call-update
  178.7 79.3 %all-gather.7.cloned.1.call-done = bf16[2,256,1024]{2,1,0:T(8,128)(2,1)} async-done(((bf16[2,16,1024]{2,1,0:T(8,128)(2,1)}), bf16[2,256,1024]{2,1,0:T(8,128)(2,1)}) %all-gather.7.cloned.1.call-update) | async-done | bytes 1048592 | tf_op jit(solution)/shard_map/all_gather | solution.py:118
  258.0 1.3 slice_bitcast_fusion.1
  259.3 2.4 fusion.36
  261.7 0.0 copy-start.1
  261.7 2.4 multiply_bitcast_fusion.1
  264.1 0.0 copy-done.1
  264.1 3.0 %fusion.11 = bf16[2,1024,1024]{2,1,0:T(8,128)(2,1)} fusion(bf16[2,1024,1024]{2,1,0:T(8,128)(2,1)S(1)} %copy-done.1, f32[1,1024,1024]{2,1,0:T(8,128)S(1)} %get-tuple-element.5, f32[1,1024,1024]{2,1,0:T(8,128)S(1)} %get-tuple-element.4), kind=kLoop, calls=%fused_computation.15 | loop fusion | flops 8388608 | bytes 16777216 | tf_op jit(solution)/shard_map/convert_element_type | solution.py:134
  (20 shorter events, 0.4 us)
Async XLA Ops:
  9.0 69.7 %all-to-all-start = ((bf16[2,16,1024]{2,0,1:T(2,128)(2,1)}), bf16[2,16,1024]{2,0,1:T(2,128)(2,1)S(1)}, u32[]{:S(2)}, u32[]{:S(2)}) async-start(bf16[2,16,1024]{2,0,1:T(2,128)(2,1)} %bitcast.141), calls=%async_computation | async-start | bytes 131072 | tf_op jit(solution)/shard_map/all_to_all | solution.py:88
  20.0 110.6 %all-gather.5.cloned.1.call-start = ((), (), s32[]{:S(2)}) async-start(), calls=%async_computation.2 | async-start | bytes 1114112 | tf_op jit(solution)/shard_map/all_gather | solution.py:118
  28.1 131.0 %all-gather.9.cloned.1.call-start = ((), (), s32[]{:S(2)}) async-start(), calls=%async_computation.4 | async-start | bytes 1114112 | tf_op jit(solution)/shard_map/all_gather | solution.py:125
  80.1 13.9 %copy-start.2 = (f32[16,1024]{1,0:T(8,128)S(1)}, f32[16,1024]{1,0:T(8,128)}, u32[]{:S(2)}) copy-start(f32[16,1024]{1,0:T(8,128)} %param.4) | copy-start | bytes 196612
  94.0 36.7 %copy-start.3 = (f32[1024]{0:T(1024)S(1)}, f32[1024]{0:T(1024)}, u32[]{:S(2)}) copy-start(f32[1024]{0:T(1024)} %param.5) | copy-start | bytes 12292
  130.6 127.4 %all-gather.7.cloned.1.call-start = ((), (), s32[]{:S(2)}) async-start(), calls=%async_computation.3 | async-start | bytes 1114112 | tf_op jit(solution)/shard_map/all_gather | solution.py:118
  165.2 2.5 copy-start
  261.7 2.5 copy-start.1
Sparse Core Ops, SparseCore 0:
  28.2 80.2 all-gather.4
  130.7 28.2 all-gather.8
  178.8 79.1 all-gather.6
